TPU v7x, 512 devices: a whole 4x8x8 slice. The times are simulated.
512 devices in a mesh: cells: 128 (over z, y_lo, x, core), stations: 4 (over y_hi).
Axes of the slice: x: 4, y: 8 (y_hi: 4, y_lo: 2; y = y_hi * 2 + y_lo), z: 8, core: 2. Of those that a mesh axis runs over, the one named last changes fastest.
Arguments:
- probes: bfloat16 [16, 524288], P(None, 'cells'), may hold values from -6 to 6
- reg_weight: float32 [524288], P('cells'), may hold values from 0.1 to 1
- cell_plan: int32 [2, 524288], P(None, 'cells'), may hold values from 0 to 255
- cell_depth: int32 [524288], P('cells'), may hold values from 0 to 15, as said below
- station_index: int32 [2, 16384], P(None, 'stations'), may hold values from 0 to 65535, as said below
- station_weight: float32 [16384], P('stations'), may hold values from 0.5 to 2
Outputs:
- basis: float32 [16, 524288], P(None, ('cells', 'stations'))
- factor: float32 [16, 16], replicated
Inputs may be any that keep to these rules, and one draw needn't show every extreme that they name: `cell_plan`: east and north cell indices of a grid of 256 by 256 columns. `cell_depth`: depth indices of 16 layers. `station_index`: east and north station positions in 1/256ths of a cell width, over the same area as the cells' grid.
All inputs are finite; a program needn't handle non-finite values.
Results may differ from a plain program's by a relative error of at most 0.00065.
Values may be sent and summed in bfloat16 or wider, within the bound.
No kernel may reach another device: no remote copies, remote signals or barrier semaphores. Data moves between devices by JAX's collectives and lax.ppermute only.
A program may use at most 64 MiB of HBM per device.

v0:
```python
import math
import jax
import jax.numpy as jnp
from jax import lax
from jax.sharding import PartitionSpec as P

GRAVITY = 2.0
JITTER = 1e-06
SUBSTEP = 0.00390625


def cell_points(cell_plan, cell_depth):
    cell_east = cell_plan[0].astype(jnp.float32) + 0.5
    cell_north = cell_plan[1].astype(jnp.float32) + 0.5
    cell_down = cell_depth.astype(jnp.float32) + 1.0
    return (cell_east, cell_north, cell_down)


def sensitivity(st_east, st_north, cell_geom):
    cell_east, cell_north, cell_down = cell_geom
    d_east = cell_east[None, :] - st_east[:, None]
    d_north = cell_north[None, :] - st_north[:, None]
    distance = d_east * d_east + d_north * d_north + cell_down[None, :] * cell_down[None, :]
    inverse = lax.rsqrt(distance)
    return (GRAVITY * cell_down[None, :] * inverse * inverse * inverse).astype(jnp.bfloat16)


def forward_terms(probes, st_east, st_north, cell_geom):
    station_count = st_east.shape[0]
    block_size = math.gcd(station_count, 512)

    def forward_advance(turn_index, running):
        start_at = turn_index * block_size
        sens_tile = sensitivity(
            lax.dynamic_slice_in_dim(st_east, start_at, block_size),
            lax.dynamic_slice_in_dim(st_north, start_at, block_size),
            cell_geom,
        )
        partial_value = lax.dot_general(
            probes, sens_tile, (((1,), (1,)), ((), ())), preferred_element_type=jnp.float32
        )
        return lax.dynamic_update_slice_in_dim(running, partial_value, start_at, 1)

    zero_field = jnp.zeros((probes.shape[0], station_count), jnp.float32)
    return lax.fori_loop(0, station_count // block_size, forward_advance, zero_field)


def transposed_add(running, weighted, st_east, st_north, cell_geom):
    station_count = weighted.shape[1]
    block_size = math.gcd(station_count, 512)

    def transposed_advance(turn_index, current):
        start_at = turn_index * block_size
        sens_tile = sensitivity(
            lax.dynamic_slice_in_dim(st_east, start_at, block_size),
            lax.dynamic_slice_in_dim(st_north, start_at, block_size),
            cell_geom,
        )
        segment = lax.dynamic_slice_in_dim(weighted, start_at, block_size, 1)
        return current + jnp.dot(segment, sens_tile, preferred_element_type=jnp.float32)

    return lax.fori_loop(0, station_count // block_size, transposed_advance, running)


def gram_term(hess_image):
    return jnp.dot(
        hess_image,
        hess_image.T,
        precision=lax.Precision.HIGHEST,
        preferred_element_type=jnp.float32,
    )


def body(probes, reg_weight, cell_plan, cell_depth, station_index, station_weight):
    cell_geom = cell_points(cell_plan, cell_depth)
    st_east = station_index[0].astype(jnp.float32) * SUBSTEP
    st_north = station_index[1].astype(jnp.float32) * SUBSTEP
    station_scale = station_weight * station_weight
    terms = forward_terms(probes, st_east, st_north, cell_geom)
    zero_image = jnp.zeros((probes.shape[0], probes.shape[1]), jnp.float32)
    station_field = lax.psum(terms, "cells")
    weighted = (station_scale[None, :] * station_field).astype(jnp.bfloat16)
    backward = transposed_add(zero_image, weighted, st_east, st_north, cell_geom)
    group_count = lax.axis_size("stations")
    quarter = probes.shape[1] // group_count
    offset_cells = lax.axis_index("stations") * quarter
    cell_total = probes.shape[1] * lax.axis_size("cells")
    summed = lax.psum(backward, "stations")
    hess_image = summed + reg_weight[None, :] * probes.astype(jnp.float32)
    gram_matrix = lax.psum(gram_term(hess_image), "cells")
    local_image = lax.dynamic_slice_in_dim(hess_image, offset_cells, quarter, 1)
    gram_matrix = gram_matrix / cell_total + JITTER * jnp.eye(probes.shape[0], dtype=jnp.float32)
    lower_factor = jnp.linalg.cholesky(gram_matrix)
    basis_rows = jax.scipy.linalg.solve_triangular(lower_factor, local_image, lower=True)
    return (basis_rows, lower_factor)


def solution(mesh):
    return jax.shard_map(
        body,
        mesh=mesh,
        in_specs=(
            P(None, "cells"),
            P("cells"),
            P(None, "cells"),
            P("cells"),
            P(None, "stations"),
            P("stations"),
        ),
        out_specs=(P(None, ("cells", "stations")), P()),
        check_vma=False,
    )
```

profile of v0, /device:TPU:16, one launch (start us, length us, event | category | flops | bytes accessed | tf_op | source)
XLA Modules:
  0.0 1378.7 jit_solution(104188721798137522)
XLA Ops:
  9.7 25.5 %while.29 = (s32[]{:T(128)}, f32[16,4096]{1,0:T(8,128)S(1)}, f32[4096]{0:T(1024)S(1)}, f32[4096]{0:T(1024)S(1)}, f32[4096]{0:T(1024)S(1)}, /*index=5*/f32[4096]{...) while((s32[]{:T(128)}, f32[16,4096]{1,0:T(8,128)S(1)}, ...), condition=%wide.region_1.0_spmd, body=%wide.region_0.0_spmd.sunk | while | flops 88084488 | bytes 274615 | solution.py:45
  9.9 3.0 fusion.35
  13.1 3.0 fusion.35
  16.3 3.0 fusion.35
  19.5 3.0 fusion.35
  22.6 3.0 fusion.35
  25.8 3.0 fusion.35
  29.0 3.0 fusion.35
  32.2 3.0 fusion.35
  36.1 966.5 %all-reduce.3.cloned.1.call-done = f32[16,4096]{1,0:T(8,128)} async-done(((f32[16,4096]{1,0:T(8,128)}), f32[16,4096]{1,0:T(8,128)}) %all-reduce.3.cloned.1.call-update) | async-done | bytes 262160 | tf_op jit(solution)/shard_map/psum | solution.py:81
  1003.5 25.6 %while.30 = (s32[]{:T(128)}, f32[16,4096]{1,0:T(8,128)S(1)}, bf16[16,4096]{1,0:T(8,128)(2,1)S(1)}, f32[4096]{0:T(1024)S(1)}, f32[4096]{0:T(1024)S(1)}, /*index=5...) while((s32[]{:T(128)}, f32[16,4096]{1,0:T(8,128)S(1)}, ...), condition=%wide.region_4.0_spmd.clone, body=%wide.region_3.0_spmd.clone.sunk | while | flops 88215560 | bytes 651457 | solution.py:62
  1003.7 3.0 convolution_add_fusion.2
  1006.9 3.0 convolution_add_fusion.2
  1010.1 3.0 convolution_add_fusion.2
  1013.3 3.0 convolution_add_fusion.2
  1016.5 3.0 convolution_add_fusion.2
  1019.7 3.0 convolution_add_fusion.2
  1022.9 3.0 convolution_add_fusion.2
  1026.1 3.0 convolution_add_fusion.2
  1029.9 51.8 %all-reduce.5.cloned.1.call-done = f32[16,4096]{1,0:T(8,128)} async-done(((f32[16,4096]{1,0:T(8,128)}), f32[16,4096]{1,0:T(8,128)}) %all-reduce.5.cloned.1.call-update) | async-done | bytes 262160 | tf_op jit(solution)/shard_map/psum | solution.py:88
  1083.1 283.1 %psum.23 = f32[16,16]{1,0:T(8,128)S(1)} all-reduce(f32[16,16]{1,0:T(8,128)S(1)} %fusion.24), channel_id=1, replica_groups=mesh['cells'=128,'stations'=4] {'cells'}, use_global_device_ids=true, to_apply=%region_6.0 | all-reduce | flops 256 | bytes 2048 | tf_op jit(solution)/shard_map/psum | solution.py:90
  1366.3 1.5 cholesky.16
  1368.5 1.2 select_bitcast_fusion
  1369.7 1.2 custom-call.7
  (77 shorter events, 10.5 us)
Async XLA Ops:
  7.2 2.6 copy-start.2
  7.2 995.4 %all-reduce.3.cloned.1.call-start = ((), (), s32[]{:S(2)}) async-start(), calls=%async_computation | async-start | bytes 524288 | tf_op jit(solution)/shard_map/psum | solution.py:81
  35.2 0.7 copy-start
  35.2 0.8 copy-start.3
  36.0 1045.7 %all-reduce.5.cloned.1.call-start = ((), (), s32[]{:S(2)}) async-start(), calls=%async_computation.1 | async-start | bytes 524288 | tf_op jit(solution)/shard_map/psum | solution.py:88
  1029.1 0.7 copy-start.1
  1029.1 52.5 %copy-start.4 = (f32[4096]{0:T(1024)S(1)}, f32[4096]{0:T(1024)}, u32[]{:S(2)}) copy-start(f32[4096]{0:T(1024)} %param.11) | copy-start | bytes 49156
Sparse Core Ops, SparseCore 0:
  36.1 966.3 all-reduce.2
  1030.0 51.6 all-reduce.4
where the time goes:
time: 1380 us
  waiting for transfers between devices  1020 us (74%)
  blocking collectives  283 us (21%)
  matrix products  50 us (4%)
  between operations  14.1 us (1%)
    psum x1, waiting for transfers between devices, body(): station_field = lax.psum(terms, 'cells')  966 us
    psum x1, blocking collectives, body(): gram_matrix = lax.psum(gram_term(hess_image), 'cells')  283 us
    psum x1, waiting for transfers between devices, body(): summed = lax.psum(backward, 'stations')  51.8 us
  transfers between devices with their start and end apart: 2, of which 2 were waited for; matrix products, arithmetic and copies ran while one was open for 0% of the time, Pallas kernels for 0%

commit v1 on v0

--- a/solution.py
+++ b/solution.py
@@ -78,7 +78,8 @@
     station_scale = station_weight * station_weight
     terms = forward_terms(probes, st_east, st_north, cell_geom)
     zero_image = jnp.zeros((probes.shape[0], probes.shape[1]), jnp.float32)
-    station_field = lax.psum(terms, "cells")
+    shards = lax.all_gather(terms, "cells", axis=0, tiled=False)
+    station_field = shards.sum(axis=0)
     weighted = (station_scale[None, :] * station_field).astype(jnp.bfloat16)
     backward = transposed_add(zero_image, weighted, st_east, st_north, cell_geom)
     group_count = lax.axis_size("stations")

time: 1380 us -> 692 us (0.50)
  waiting for transfers between devices: 1020 us -> 313 us
    psum x1 -> x0, waiting for transfers between devices: 966 us -> none  [body(): station_field = lax.psum(terms, 'cells')]
    all_gather x0 -> x1, waiting for transfers between devices: none -> 259 us  [body(): shards = lax.all_gather(terms, 'cells', axis=0, tiled=False)]
where the time goes in v1:
time: 692 us; the launch traced here: 691 us
  waiting for transfers between devices  313 us (45%)
  blocking collectives  283 us (41%)
  matrix products  57.2 us (8%)
  other arithmetic  20 us (3%)
  between operations  14.1 us (2%)
    psum x1, blocking collectives, body(): gram_matrix = lax.psum(gram_term(hess_image), 'cells')  283 us
    all_gather x1, waiting for transfers between devices, body(): shards = lax.all_gather(terms, 'cells', axis=0, tiled=False)  259 us
    psum x1, waiting for transfers between devices, body(): summed = lax.psum(backward, 'stations')  53.2 us
    dot_general x8, matrix products, forward_advance(): lax.dot_general(probes, sens_tile, (((1,), (1,)), ((), ())), preferred_el...  31.5 us
    dot_general x8, matrix products, transposed_advance(): jnp.dot(segment, sens_tile, preferred_element_type=jnp.float32)  24.4 us
  transfers between devices with their start and end apart: 2, of which 2 were waited for; matrix products, arithmetic and copies ran while one was open for 0% of the time, Pallas kernels for 0%

profile of v1, /device:TPU:16, one launch (start us, length us, event | category | flops | bytes accessed | tf_op | source)
XLA Modules:
  0.0 691.3 jit_solution(2072303943453521960)
XLA Ops:
  9.7 32.7 %while.29 = (s32[]{:T(128)}, f32[16,4096]{1,0:T(8,128)S(1)}, f32[4096]{0:T(1024)S(1)}, f32[4096]{0:T(1024)S(1)}, f32[4096]{0:T(1024)S(1)}, /*index=5*/f32[4096]{...) while((s32[]{:T(128)}, f32[16,4096]{1,0:T(8,128)S(1)}, ...), condition=%wide.region_1.0_spmd, body=%wide.region_0.0_spmd.sunk | while | flops 88084488 | bytes 274615 | solution.py:45
  9.9 3.9 fusion.35
  14.0 3.9 fusion.35
  18.1 3.9 fusion.35
  22.2 3.9 fusion.35
  26.2 3.9 fusion.35
  30.3 3.9 fusion.35
  34.4 3.9 fusion.35
  38.5 3.9 fusion.35
  43.3 259.5 %all-gather.3.cloned.1.call-done = f32[2048,4096]{1,0:T(8,128)} async-done(((f32[16,4096]{1,0:T(8,128)}), f32[2048,4096]{1,0:T(8,128)}) %all-gather.3.cloned.1.call-update) | async-done | bytes 33554448 | tf_op jit(solution)/shard_map/all_gather | solution.py:81
  302.8 11.9 %reduce_sum.9 = f32[16,4096]{1,0:T(8,128)S(1)} reduce(f32[128,16,4096]{2,1,0:T(8,128)} %bitcast.32, f32[]{:T(128)} %constant.137.clone.1), dimensions={0}, to_apply=%region_2.0 | reduce | flops 8323072 | bytes 33816580 | tf_op jit(solution)/shard_map/reduce_sum | solution.py:82
  314.7 25.6 %while.30 = (s32[]{:T(128)}, f32[16,4096]{1,0:T(8,128)S(1)}, bf16[16,4096]{1,0:T(8,128)(2,1)S(1)}, f32[4096]{0:T(1024)S(1)}, f32[4096]{0:T(1024)S(1)}, /*index=5...) while((s32[]{:T(128)}, f32[16,4096]{1,0:T(8,128)S(1)}, ...), condition=%wide.region_4.0_spmd.clone, body=%wide.region_3.0_spmd.clone.sunk | while | flops 88215560 | bytes 651457 | solution.py:62
  314.9 3.0 convolution_add_fusion.2
  318.1 3.0 convolution_add_fusion.2
  321.3 3.0 convolution_add_fusion.2
  324.5 3.0 convolution_add_fusion.2
  327.7 3.0 convolution_add_fusion.2
  330.9 3.0 convolution_add_fusion.2
  334.1 3.0 convolution_add_fusion.2
  337.3 3.0 convolution_add_fusion.2
  341.1 53.2 %all-reduce.2.cloned.1.call-done = f32[16,4096]{1,0:T(8,128)} async-done(((f32[16,4096]{1,0:T(8,128)}), f32[16,4096]{1,0:T(8,128)}) %all-reduce.2.cloned.1.call-update) | async-done | bytes 262160 | tf_op jit(solution)/shard_map/psum | solution.py:89
  395.7 283.1 %psum.15 = f32[16,16]{1,0:T(8,128)S(1)} all-reduce(f32[16,16]{1,0:T(8,128)S(1)} %fusion.24), channel_id=1, replica_groups=mesh['cells'=128,'stations'=4] {'cells'}, use_global_device_ids=true, to_apply=%region_6.0 | all-reduce | flops 256 | bytes 2048 | tf_op jit(solution)/shard_map/psum | solution.py:91
  678.9 1.5 cholesky.16
  681.0 1.2 select_bitcast_fusion
  (78 shorter events, 10.8 us)
Async XLA Ops:
  7.2 295.6 %all-gather.3.cloned.1.call-start = ((), (), s32[]{:S(2)}) async-start(), calls=%async_computation.1 | async-start | bytes 33816576 | tf_op jit(solution)/shard_map/all_gather | solution.py:81
  9.7 33.6 %copy-start.3 = (f32[4096]{0:T(1024)S(1)}, f32[4096]{0:T(1024)}, u32[]{:S(2)}) copy-start(f32[4096]{0:T(1024)} %param.15) | copy-start | bytes 49156
  42.5 0.7 copy-start
  43.2 351.0 %all-reduce.2.cloned.1.call-start = ((), (), s32[]{:S(2)}) async-start(), calls=%async_computation | async-start | bytes 524288 | tf_op jit(solution)/shard_map/psum | solution.py:89
  314.7 79.6 %copy-start.2 = (bf16[16,4096]{1,0:T(8,128)(2,1)S(1)}, bf16[16,4096]{1,0:T(8,128)(2,1)}, u32[]{:S(2)}) copy-start(bf16[16,4096]{1,0:T(8,128)(2,1)} %get-tuple-element.627) | copy-start | bytes 393220
  314.7 79.6 %copy-start.4 = (f32[4096]{0:T(1024)S(1)}, f32[4096]{0:T(1024)}, u32[]{:S(2)}) copy-start(f32[4096]{0:T(1024)} %param.11) | copy-start | bytes 49156
  340.3 0.7 copy-start.1
Sparse Core Ops, SparseCore 0:
  43.3 259.4 all-gather.2
  341.2 53.0 all-reduce.1
